TPU v7x, 32 devices: a whole 2x2x4 slice. The times are simulated.
32 devices in a mesh: depth: 8 (over y, x, core), dp: 4 (over z).
Axes of the slice: x: 2, y: 2, z: 4, core: 2. Of those that a mesh axis runs over, the one named last changes fastest.
Arguments:
- token_ids: int32 [512], P('dp'), may hold values from 0 to 10239
- embedding: bfloat16 [10240, 512], P('depth'), may hold values from -6 to 6
- w_up: bfloat16 [16, 512, 2048], P('depth'), may hold values from -0.25 to 0.25
- w_down: bfloat16 [16, 2048, 512], P('depth'), may hold values from -0.125 to 0.125
- cotangent: bfloat16 [512, 512], P('dp'), may hold values from -0.119628906 to 0.119628906
Outputs:
- grad_up: float32 [16, 512, 2048], P('depth', 'dp')
- grad_down: float32 [16, 2048, 512], P('depth', 'dp')
All inputs are finite; a program needn't handle non-finite values.
Results may differ from a plain program's by a relative error of at most 0.03.
Values may be sent and summed in bfloat16 or wider, within the bound.
No kernel may reach another device: no remote copies, remote signals or barrier semaphores. Data moves between devices by JAX's collectives and lax.ppermute only.
A program may use at most 64 MiB of HBM per device.

v0:
```python
import jax
import jax.numpy as jnp
from jax import lax
from jax.sharding import PartitionSpec as P

RELAX = 3
EPSILON = 1e-06
GAMMA = 0.05


def shifted(block, axis, distance):
    devices = range(lax.axis_size(axis))
    route = [(i - distance, i) for i in devices if i - distance in devices]
    return lax.ppermute(block, axis, route)


def layer_forward(state, weight_up, weight_down):
    scale = lax.rsqrt(jnp.mean(state * state, axis=-1, keepdims=True) + EPSILON)
    normed = (state * scale).astype(jnp.bfloat16)
    before = jnp.dot(normed, weight_up, preferred_element_type=jnp.float32)
    hidden = jax.nn.silu(before).astype(jnp.bfloat16)
    output = state + jnp.dot(hidden, weight_down, preferred_element_type=jnp.float32)
    return (output, (scale, normed, before, hidden))


def layer_adjoint(state, saved, adjoint, weight_up, weight_down):
    scale, normed, before, hidden = saved
    adjoint_low = adjoint.astype(jnp.bfloat16)
    toward_hidden = lax.dot_general(
        adjoint_low, weight_down, (((1,), (1,)), ((), ())), preferred_element_type=jnp.float32
    )
    sigma = jax.nn.sigmoid(before)
    delta = (toward_hidden * sigma * (1.0 + before * (1.0 - sigma))).astype(jnp.bfloat16)
    toward_normed = lax.dot_general(
        delta, weight_up, (((1,), (1,)), ((), ())), preferred_element_type=jnp.float32
    )
    unit = state * scale
    inner = jnp.mean(toward_normed * unit, axis=-1, keepdims=True)
    return (adjoint + scale * (toward_normed - unit * inner), adjoint_low, delta)


def coarse_matrix(weight_up, weight_down):
    total = jnp.dot(weight_up[0], weight_down[0], preferred_element_type=jnp.float32)
    total = total + jnp.dot(weight_up[1], weight_down[1], preferred_element_type=jnp.float32)
    return jnp.eye(weight_up.shape[1], dtype=jnp.float32) + GAMMA * total


def shards(token_ids, embedding, w_up, w_down, cotangent):
    depth = lax.axis_size("depth")
    position = lax.axis_index("depth")
    first = position == 0
    final_block = position == depth - 1
    layers = w_up.shape[0]
    vocab_rows = embedding.shape[0]
    local_ids = token_ids - position * vocab_rows
    inside = (local_ids >= 0) & (local_ids < vocab_rows)
    picked = jnp.take(embedding, jnp.clip(local_ids, 0, vocab_rows - 1), axis=0)
    picked = jnp.where(inside[:, None], picked, jnp.zeros_like(picked)).astype(jnp.float32)
    start = lax.psum(picked.astype(jnp.bfloat16), "depth").astype(jnp.float32)
    matrix = coarse_matrix(w_up, w_down)
    transposed = matrix.T
    zeros = jnp.zeros_like(start)
    coarse = start
    arrived_projection = zeros
    for sweep in range(RELAX):
        run_state = coarse
        for run_layer in range(layers):
            run_state, unused = layer_forward(run_state, w_up[run_layer], w_down[run_layer])
        projection = jnp.dot(coarse, matrix, precision=lax.Precision.HIGHEST)
        arrived, arrived_projection = shifted((run_state, projection), "depth", 1)
        coarse = jnp.where(first, start, arrived)
    tau = coarse - arrived_projection

    def forward_turn(turn, incoming):
        carried = jnp.dot(incoming + tau, matrix, precision=lax.Precision.HIGHEST)
        return shifted(carried.astype(jnp.bfloat16), "depth", 1).astype(carried.dtype)

    incoming = lax.fori_loop(0, depth - 1, forward_turn, zeros)
    corrected = incoming + tau
    states = []
    saves = []
    state = corrected
    for layer in range(layers):
        states.append(state)
        state, saved = layer_forward(state, w_up[layer], w_down[layer])
        saves.append(saved)

    def run_adjoint(adjoint):
        for layer in reversed(range(layers)):
            adjoint, low, delta = layer_adjoint(
                states[layer], saves[layer], adjoint, w_up[layer], w_down[layer]
            )
        return adjoint

    final = cotangent.astype(jnp.float32)
    adjoint_state = final
    back_projection = zeros
    for sweep in range(RELAX):
        begun = run_adjoint(adjoint_state)
        projection = jnp.dot(adjoint_state, transposed, precision=lax.Precision.HIGHEST)
        arrived, back_projection = (
            shifted(begun.astype(jnp.bfloat16), "depth", -1).astype(begun.dtype),
            shifted(projection.astype(jnp.bfloat16), "depth", -1).astype(projection.dtype),
        )
        adjoint_state = jnp.where(final_block, final, arrived)
    back_tau = adjoint_state - back_projection

    def backward_turn(turn, incoming):
        carried = jnp.dot(incoming + back_tau, transposed, precision=lax.Precision.HIGHEST)
        return shifted(carried.astype(jnp.bfloat16), "depth", -1).astype(carried.dtype)

    back_incoming = lax.fori_loop(0, depth - 1, backward_turn, zeros)
    adjoint = back_incoming + back_tau
    lows = [None] * layers
    deltas = [None] * layers
    for layer in reversed(range(layers)):
        adjoint, low, delta = layer_adjoint(
            states[layer], saves[layer], adjoint, w_up[layer], w_down[layer]
        )
        lows[layer] = low
        deltas[layer] = delta
    normed_all = jnp.stack([saves[layer][1] for layer in range(layers)], 0)
    hidden_all = jnp.stack([saves[layer][3] for layer in range(layers)], 0)
    delta_all = jnp.stack(deltas, 0)
    low_all = jnp.stack(lows, 0)
    normed_part, hidden_part = (
        lax.all_to_all(normed_all, "dp", split_axis=2, concat_axis=1, tiled=True),
        lax.all_to_all(hidden_all, "dp", split_axis=2, concat_axis=1, tiled=True),
    )
    delta_whole, low_whole = (
        lax.all_gather(delta_all, "dp", axis=1, tiled=True),
        lax.all_gather(low_all, "dp", axis=1, tiled=True),
    )
    grad_up = jnp.einsum(
        "ltd,ltf->ldf", normed_part, delta_whole, preferred_element_type=jnp.float32
    )
    grad_down = jnp.einsum(
        "ltf,ltd->lfd", hidden_part, low_whole, preferred_element_type=jnp.float32
    )
    return (grad_up, grad_down)


def solution(mesh):
    in_specs = (
        P("dp"),
        P("depth", None),
        P("depth", None, None),
        P("depth", None, None),
        P("dp", None),
    )
    out_specs = (P("depth", "dp", None), P("depth", "dp", None))
    return jax.shard_map(shards, mesh=mesh, in_specs=in_specs, out_specs=out_specs, check_vma=False)
```

profile of v0, /device:TPU:0, one launch (start us, length us, event | category | flops | bytes accessed | tf_op | source)
XLA Modules:
  0.0 437.5 jit_solution(14068713169038172877)
XLA Ops:
  10.2 57.6 %all-reduce.2.cloned.1.call-done = bf16[128,512]{1,0:T(8,128)(2,1)} async-done(((bf16[128,512]{1,0:T(8,128)(2,1)}), bf16[128,512]{1,0:T(8,128)(2,1)}) %all-reduce.2.cloned.1.call-update) | async-done | bytes 131088 | tf_op jit(solution)/shard_map/psum | solution.py:59
  68.8 3.1 multiply_reduce_fusion.13
  71.9 3.0 fusion.115
  75.0 1.4 collective-permute-start.2
  76.4 4.4 %fusion.27 = f32[512,512]{1,0:T(8,128)} fusion(bf16[2,2048,512]{2,1,0:T(8,128)(2,1)} %param.12, bf16[2,512,2048]{2,1,0:T(8,128)(2,1)} %param.11), kind=kOutput, calls=%fused_computation.40 | convolution fusion | flops 1073741824 | bytes 5242880 | tf_op jit(solution)/shard_map/dot_general | solution.py:44
  81.0 3.1 multiply_reduce_fusion.11
  84.1 3.7 fusion.118
  87.8 3.5 collective-permute-start.3
  91.3 3.7 convert_add_fusion
  95.9 3.7 multiply_reduce_fusion.9
  99.7 4.0 fusion.121
  103.6 4.0 collective-permute-start.4
  107.6 1.5 fusion.244
  109.1 4.5 %collective-permute-start.5 = (f32[128,512]{1,0:T(8,128)}, f32[128,512]{1,0:T(8,128)S(1)}, u32[]{:S(2)}, u32[]{:S(2)}) collective-permute-start(f32[128,512]{1,0:T(8,128)} %fusion.244), channel_id=1, source_target_pairs={{0,4},{4,8},{8,12},{12,16},{16,20},{20,24},{24,28},{1,5},{5,9},{9,... | collective-permute-start | bytes 786440 | tf_op jit(solution)/shard_map/ppermute | solution.py:14
  114.8 50.3 %while.22 = (s32[]{:T(128)}, f32[128,512]{1,0:T(8,128)S(1)}, f32[128,512]{1,0:T(8,128)S(1)}, f32[512,512]{1,0:T(8,128)S(1)}, s32[]{:T(128)}, /*index=5*/s32[]{:T(128)}) while((s32[]{:T(128)}, f32[128,512]{1,0:T(8,128)S(1)}, f32[128,512]{1,0:T(8,128)S(1)}, f32[512,512]{1,0:T(8,128)S(1)}, s32[]{:T(128)}, /*index=5*/s32[]{:T(128)}) %tuple.64), condition=%wide.region_8.9_spmd.clone, body=%wide.region_7.8_spmd.clone.sunk | while | flops 402915328 | bytes 2621559 | solution.py:78
  115.6 5.4 %collective-permute-start = (bf16[128,512]{1,0:T(8,128)(2,1)S(1)}, bf16[128,512]{1,0:T(8,128)(2,1)S(1)}, u32[]{:S(2)}, u32[]{:S(2)}) collective-permute-start(bf16[128,512]{1,0:T(8,128)(2,1)S(1)} %convolution_convert_fusion.5), channel_id=1, source_target_pairs={{0,4},{4,8},{8,12},{12,16},{16,20},{20,24},{24,28},{1,5},{5,9},{9,... | collective-permute-start | bytes 393224 | tf_op jit(solution)/shard_map/while/body/eval_jaxpr/ppermute | solution.py:14
  122.8 5.2 %collective-permute-start = (bf16[128,512]{1,0:T(8,128)(2,1)S(1)}, bf16[128,512]{1,0:T(8,128)(2,1)S(1)}, u32[]{:S(2)}, u32[]{:S(2)}) collective-permute-start(bf16[128,512]{1,0:T(8,128)(2,1)S(1)} %convolution_convert_fusion.5), channel_id=1, source_target_pairs={{0,4},{4,8},{8,12},{12,16},{16,20},{20,24},{24,28},{1,5},{5,9},{9,... | collective-permute-start | bytes 393224 | tf_op jit(solution)/shard_map/while/body/eval_jaxpr/ppermute | solution.py:14
  129.8 5.3 %collective-permute-start = (bf16[128,512]{1,0:T(8,128)(2,1)S(1)}, bf16[128,512]{1,0:T(8,128)(2,1)S(1)}, u32[]{:S(2)}, u32[]{:S(2)}) collective-permute-start(bf16[128,512]{1,0:T(8,128)(2,1)S(1)} %convolution_convert_fusion.5), channel_id=1, source_target_pairs={{0,4},{4,8},{8,12},{12,16},{16,20},{20,24},{24,28},{1,5},{5,9},{9,... | collective-permute-start | bytes 393224 | tf_op jit(solution)/shard_map/while/body/eval_jaxpr/ppermute | solution.py:14
  136.8 5.3 %collective-permute-start = (bf16[128,512]{1,0:T(8,128)(2,1)S(1)}, bf16[128,512]{1,0:T(8,128)(2,1)S(1)}, u32[]{:S(2)}, u32[]{:S(2)}) collective-permute-start(bf16[128,512]{1,0:T(8,128)(2,1)S(1)} %convolution_convert_fusion.5), channel_id=1, source_target_pairs={{0,4},{4,8},{8,12},{12,16},{16,20},{20,24},{24,28},{1,5},{5,9},{9,... | collective-permute-start | bytes 393224 | tf_op jit(solution)/shard_map/while/body/eval_jaxpr/ppermute | solution.py:14
  143.9 5.3 %collective-permute-start = (bf16[128,512]{1,0:T(8,128)(2,1)S(1)}, bf16[128,512]{1,0:T(8,128)(2,1)S(1)}, u32[]{:S(2)}, u32[]{:S(2)}) collective-permute-start(bf16[128,512]{1,0:T(8,128)(2,1)S(1)} %convolution_convert_fusion.5), channel_id=1, source_target_pairs={{0,4},{4,8},{8,12},{12,16},{16,20},{20,24},{24,28},{1,5},{5,9},{9,... | collective-permute-start | bytes 393224 | tf_op jit(solution)/shard_map/while/body/eval_jaxpr/ppermute | solution.py:14
  151.0 5.3 %collective-permute-start = (bf16[128,512]{1,0:T(8,128)(2,1)S(1)}, bf16[128,512]{1,0:T(8,128)(2,1)S(1)}, u32[]{:S(2)}, u32[]{:S(2)}) collective-permute-start(bf16[128,512]{1,0:T(8,128)(2,1)S(1)} %convolution_convert_fusion.5), channel_id=1, source_target_pairs={{0,4},{4,8},{8,12},{12,16},{16,20},{20,24},{24,28},{1,5},{5,9},{9,... | collective-permute-start | bytes 393224 | tf_op jit(solution)/shard_map/while/body/eval_jaxpr/ppermute | solution.py:14
  158.1 6.1 %collective-permute-start = (bf16[128,512]{1,0:T(8,128)(2,1)S(1)}, bf16[128,512]{1,0:T(8,128)(2,1)S(1)}, u32[]{:S(2)}, u32[]{:S(2)}) collective-permute-start(bf16[128,512]{1,0:T(8,128)(2,1)S(1)} %convolution_convert_fusion.5), channel_id=1, source_target_pairs={{0,4},{4,8},{8,12},{12,16},{16,20},{20,24},{24,28},{1,5},{5,9},{9,... | collective-permute-start | bytes 393224 | tf_op jit(solution)/shard_map/while/body/eval_jaxpr/ppermute | solution.py:14
  165.3 2.2 fusion.72
  168.7 1.9 copy-done.6
  170.6 1.5 fusion.43
  172.0 4.2 multiply_reduce_fusion.6
  176.2 3.9 multiply_reduce_fusion.5
  180.3 1.3 collective-permute-start.6
  181.6 5.7 %collective-permute-done.6 = bf16[128,512]{1,0:T(8,128)(2,1)S(1)} collective-permute-done((bf16[128,512]{1,0:T(8,128)(2,1)S(1)}, bf16[128,512]{1,0:T(8,128)(2,1)S(1)}, u32[]{:S(2)}, u32[]{:S(2)}) %collective-permute-start.6) | collective-permute-done | bytes 131104 | tf_op jit(solution)/shard_map/ppermute | solution.py:14
  187.4 4.2 multiply_reduce_fusion.4
  191.7 4.3 multiply_reduce_fusion.3
  196.1 1.3 collective-permute-start.7
  197.4 6.6 %collective-permute-done.7 = bf16[128,512]{1,0:T(8,128)(2,1)S(1)} collective-permute-done((bf16[128,512]{1,0:T(8,128)(2,1)S(1)}, bf16[128,512]{1,0:T(8,128)(2,1)S(1)}, u32[]{:S(2)}, u32[]{:S(2)}) %collective-permute-start.7) | collective-permute-done | bytes 131104 | tf_op jit(solution)/shard_map/ppermute | solution.py:14
  204.0 1.8 convolution_convert_fusion.2
  207.1 4.8 %multiply_reduce_fusion.2 = (f32[128]{0:T(128)S(1)}, f32[128,512]{1,0:T(8,128)}) fusion(f32[128,512]{1,0:T(8,128)S(1)} %get-tuple-element.122, f32[128]{0:T(128)S(1)} %add_rsqrt_fusion, bf16[2,512,2048]{2,1,0:T(8,128)(2,1)} %param.11, f32[128,2048]{1,0:T(8,128)} %fusion.43, bf16[2,2048,512]{2,1,0:T(8,128)(2,1)} %param.12, ...), kind=kOutput, calls=%fused_computation.173 | convolution fusion | flops 539688832 | bytes 6030337 | tf_op jit(solution)/shard_map/dot_general | solution.py:34
  213.0 4.2 multiply_reduce_fusion.1
  218.0 1.5 collective-permute-start.8
  220.6 1.6 copy.12
  222.2 3.7 collective-permute-done.8
  226.9 56.5 %while.23 = (s32[]{:T(128)}, f32[128,512]{1,0:T(8,128)S(1)}, f32[128,512]{1,0:T(8,128)S(1)}, f32[512,512]{1,0:T(8,128)S(1)}, s32[]{:T(128)}, /*index=5*/s32[]{:T(128)}) while((s32[]{:T(128)}, f32[128,512]{1,0:T(8,128)S(1)}, f32[128,512]{1,0:T(8,128)S(1)}, f32[512,512]{1,0:T(8,128)S(1)}, s32[]{:T(128)}, ...), condition=%wide.region_18.19_spmd.clone, body=%wide.region_17.18_spmd.clone.sunk | while | flops 402915328 | bytes 2621559 | solution.py:112
  227.6 1.3 collective-permute-start.1
  228.9 6.6 %collective-permute-done.1 = bf16[128,512]{1,0:T(8,128)(2,1)S(1)} collective-permute-done((bf16[128,512]{1,0:T(8,128)(2,1)S(1)}, bf16[128,512]{1,0:T(8,128)(2,1)S(1)}, u32[]{:S(2)}, u32[]{:S(2)}) %collective-permute-start.1) | collective-permute-done | bytes 131104 | tf_op jit(solution)/shard_map/while/body/eval_jaxpr/ppermute | solution.py:14
  236.3 1.3 collective-permute-start.1
  237.6 5.9 %collective-permute-done.1 = bf16[128,512]{1,0:T(8,128)(2,1)S(1)} collective-permute-done((bf16[128,512]{1,0:T(8,128)(2,1)S(1)}, bf16[128,512]{1,0:T(8,128)(2,1)S(1)}, u32[]{:S(2)}, u32[]{:S(2)}) %collective-permute-start.1) | collective-permute-done | bytes 131104 | tf_op jit(solution)/shard_map/while/body/eval_jaxpr/ppermute | solution.py:14
  244.3 1.3 collective-permute-start.1
  245.6 5.9 %collective-permute-done.1 = bf16[128,512]{1,0:T(8,128)(2,1)S(1)} collective-permute-done((bf16[128,512]{1,0:T(8,128)(2,1)S(1)}, bf16[128,512]{1,0:T(8,128)(2,1)S(1)}, u32[]{:S(2)}, u32[]{:S(2)}) %collective-permute-start.1) | collective-permute-done | bytes 131104 | tf_op jit(solution)/shard_map/while/body/eval_jaxpr/ppermute | solution.py:14
  252.2 1.3 collective-permute-start.1
  253.5 5.9 %collective-permute-done.1 = bf16[128,512]{1,0:T(8,128)(2,1)S(1)} collective-permute-done((bf16[128,512]{1,0:T(8,128)(2,1)S(1)}, bf16[128,512]{1,0:T(8,128)(2,1)S(1)}, u32[]{:S(2)}, u32[]{:S(2)}) %collective-permute-start.1) | collective-permute-done | bytes 131104 | tf_op jit(solution)/shard_map/while/body/eval_jaxpr/ppermute | solution.py:14
  261.5 5.9 %collective-permute-done.1 = bf16[128,512]{1,0:T(8,128)(2,1)S(1)} collective-permute-done((bf16[128,512]{1,0:T(8,128)(2,1)S(1)}, bf16[128,512]{1,0:T(8,128)(2,1)S(1)}, u32[]{:S(2)}, u32[]{:S(2)}) %collective-permute-start.1) | collective-permute-done | bytes 131104 | tf_op jit(solution)/shard_map/while/body/eval_jaxpr/ppermute | solution.py:14
  269.5 5.9 %collective-permute-done.1 = bf16[128,512]{1,0:T(8,128)(2,1)S(1)} collective-permute-done((bf16[128,512]{1,0:T(8,128)(2,1)S(1)}, bf16[128,512]{1,0:T(8,128)(2,1)S(1)}, u32[]{:S(2)}, u32[]{:S(2)}) %collective-permute-start.1) | collective-permute-done | bytes 131104 | tf_op jit(solution)/shard_map/while/body/eval_jaxpr/ppermute | solution.py:14
  276.1 1.3 collective-permute-start.1
  277.4 5.9 %collective-permute-done.1 = bf16[128,512]{1,0:T(8,128)(2,1)S(1)} collective-permute-done((bf16[128,512]{1,0:T(8,128)(2,1)S(1)}, bf16[128,512]{1,0:T(8,128)(2,1)S(1)}, u32[]{:S(2)}, u32[]{:S(2)}) %collective-permute-start.1) | collective-permute-done | bytes 131104 | tf_op jit(solution)/shard_map/while/body/eval_jaxpr/ppermute | solution.py:14
  283.4 2.9 fusion.20
  289.1 2.5 fusion.22
  292.7 1.6 pad_maximum_fusion.2
  294.3 1.8 copy.10
  296.1 4.6 %all-to-all-start = ((bf16[2,128,512]{1,0,2:T(2,128)(2,1)}), bf16[2,128,512]{1,0,2:T(2,128)(2,1)}, u32[]{:S(2)}, u32[]{:S(2)}) async-start(bf16[2,128,512]{1,0,2:T(2,128)(2,1)} %copy.10), calls=%async_computation | async-start | bytes 524288 | tf_op jit(solution)/shard_map/all_to_all | solution.py:127
  301.4 2.0 copy.13
  303.4 4.2 all-to-all-done
  307.6 3.5 all-to-all-start.1
  313.1 37.0 %all-to-all-done.1 = bf16[2,128,2048]{1,0,2:T(2,128)(2,1)S(1)} async-done(((bf16[2,128,2048]{1,0,2:T(2,128)(2,1)}), bf16[2,128,2048]{1,0,2:T(2,128)(2,1)S(1)}, u32[]{:S(2)}, u32[]{:S(2)}) %all-to-all-start.1) | async-done | bytes 1048608 | tf_op jit(solution)/shard_map/all_to_all | solution.py:128
  351.4 3.4 fusion.292
  354.8 72.0 %all-gather.3.cloned.1.call-done = bf16[2,512,2048]{2,1,0:T(8,128)(2,1)} async-done(((bf16[2,128,2048]{2,1,0:T(8,128)(2,1)}), bf16[2,512,2048]{2,1,0:T(8,128)(2,1)}) %all-gather.3.cloned.1.call-update) | async-done | bytes 4194320 | tf_op jit(solution)/shard_map/all_gather | solution.py:131
  426.8 4.2 fusion.291
  (126 shorter events, 40.7 us)
Async XLA Ops:
  7.2 1.3 copy-start
  7.2 60.6 %all-reduce.2.cloned.1.call-start = ((), (), s32[]{:S(2)}) async-start(), calls=%async_computation.2 | async-start | bytes 262144 | tf_op jit(solution)/shard_map/psum | solution.py:59
  10.1 341.2 %all-gather.5.cloned.1.call-start = ((), (), s32[]{:S(2)}) async-start(), calls=%async_computation.4 | async-start | bytes 1310720 | tf_op jit(solution)/shard_map/all_gather | solution.py:132
  75.0 5.9 %copy-start.9 = (bf16[128,512]{1,0:T(8,128)(2,1)S(1)}, bf16[128,512]{1,0:T(8,128)(2,1)}, u32[]{:S(2)}) copy-start(bf16[128,512]{1,0:T(8,128)(2,1)} %all-reduce.2.cloned.1.call-done) | copy-start | bytes 393220
  75.0 5.9 %collective-permute-start.2 = (f32[128,512]{1,0:T(8,128)S(1)}, f32[128,512]{1,0:T(8,128)S(1)}, u32[]{:S(2)}, u32[]{:S(2)}) collective-permute-start(f32[128,512]{1,0:T(8,128)S(1)} %fusion.115), channel_id=1, source_target_pairs={{0,4},{4,8},{8,12},{12,16},{16,20},{20,24},{24,28},{1,5},{5,9},{9,... | collective-permute-start | bytes 786440 | tf_op jit(solution)/shard_map/ppermute | solution.py:14
  87.8 7.2 %collective-permute-start.3 = (f32[128,512]{1,0:T(8,128)}, f32[128,512]{1,0:T(8,128)S(1)}, u32[]{:S(2)}, u32[]{:S(2)}) collective-permute-start(f32[128,512]{1,0:T(8,128)} %fusion.118), channel_id=1, source_target_pairs={{0,4},{4,8},{8,12},{12,16},{16,20},{20,24},{24,28},{1,5},{5,9},{9,... | collective-permute-start | bytes 786440 | tf_op jit(solution)/shard_map/ppermute | solution.py:14
  95.0 12.6 %copy-start.1 = (f32[512,512]{1,0:T(8,128)}, f32[512,512]{1,0:T(8,128)S(1)}, u32[]{:S(2)}) copy-start(f32[512,512]{1,0:T(8,128)S(1)} %get-tuple-element.120) | copy-start | bytes 3145732
  95.1 0.8 copy-start.11
  103.6 10.0 %collective-permute-start.4 = (f32[128,512]{1,0:T(8,128)}, f32[128,512]{1,0:T(8,128)}, u32[]{:S(2)}, u32[]{:S(2)}) collective-permute-start(f32[128,512]{1,0:T(8,128)} %fusion.121), channel_id=1, source_target_pairs={{0,4},{4,8},{8,12},{12,16},{16,20},{20,24},{24,28},{1,5},{5,9},{9,... | collective-permute-start | bytes 786440 | tf_op jit(solution)/shard_map/ppermute | solution.py:14
  109.1 5.7 %collective-permute-start.5 = (f32[128,512]{1,0:T(8,128)}, f32[128,512]{1,0:T(8,128)S(1)}, u32[]{:S(2)}, u32[]{:S(2)}) collective-permute-start(f32[128,512]{1,0:T(8,128)} %fusion.244), channel_id=1, source_target_pairs={{0,4},{4,8},{8,12},{12,16},{16,20},{20,24},{24,28},{1,5},{5,9},{9,... | collective-permute-start | bytes 786440 | tf_op jit(solution)/shard_map/ppermute | solution.py:14
  115.6 6.4 %collective-permute-start = (bf16[128,512]{1,0:T(8,128)(2,1)S(1)}, bf16[128,512]{1,0:T(8,128)(2,1)S(1)}, u32[]{:S(2)}, u32[]{:S(2)}) collective-permute-start(bf16[128,512]{1,0:T(8,128)(2,1)S(1)} %convolution_convert_fusion.5), channel_id=1, source_target_pairs={{0,4},{4,8},{8,12},{12,16},{16,20},{20,24},{24,28},{1,5},{5,9},{9,... | collective-permute-start | bytes 393224 | tf_op jit(solution)/shard_map/while/body/eval_jaxpr/ppermute | solution.py:14
  122.8 6.2 %collective-permute-start = (bf16[128,512]{1,0:T(8,128)(2,1)S(1)}, bf16[128,512]{1,0:T(8,128)(2,1)S(1)}, u32[]{:S(2)}, u32[]{:S(2)}) collective-permute-start(bf16[128,512]{1,0:T(8,128)(2,1)S(1)} %convolution_convert_fusion.5), channel_id=1, source_target_pairs={{0,4},{4,8},{8,12},{12,16},{16,20},{20,24},{24,28},{1,5},{5,9},{9,... | collective-permute-start | bytes 393224 | tf_op jit(solution)/shard_map/while/body/eval_jaxpr/ppermute | solution.py:14
  129.8 6.3 %collective-permute-start = (bf16[128,512]{1,0:T(8,128)(2,1)S(1)}, bf16[128,512]{1,0:T(8,128)(2,1)S(1)}, u32[]{:S(2)}, u32[]{:S(2)}) collective-permute-start(bf16[128,512]{1,0:T(8,128)(2,1)S(1)} %convolution_convert_fusion.5), channel_id=1, source_target_pairs={{0,4},{4,8},{8,12},{12,16},{16,20},{20,24},{24,28},{1,5},{5,9},{9,... | collective-permute-start | bytes 393224 | tf_op jit(solution)/shard_map/while/body/eval_jaxpr/ppermute | solution.py:14
  136.8 6.3 %collective-permute-start = (bf16[128,512]{1,0:T(8,128)(2,1)S(1)}, bf16[128,512]{1,0:T(8,128)(2,1)S(1)}, u32[]{:S(2)}, u32[]{:S(2)}) collective-permute-start(bf16[128,512]{1,0:T(8,128)(2,1)S(1)} %convolution_convert_fusion.5), channel_id=1, source_target_pairs={{0,4},{4,8},{8,12},{12,16},{16,20},{20,24},{24,28},{1,5},{5,9},{9,... | collective-permute-start | bytes 393224 | tf_op jit(solution)/shard_map/while/body/eval_jaxpr/ppermute | solution.py:14
  143.9 6.3 %collective-permute-start = (bf16[128,512]{1,0:T(8,128)(2,1)S(1)}, bf16[128,512]{1,0:T(8,128)(2,1)S(1)}, u32[]{:S(2)}, u32[]{:S(2)}) collective-permute-start(bf16[128,512]{1,0:T(8,128)(2,1)S(1)} %convolution_convert_fusion.5), channel_id=1, source_target_pairs={{0,4},{4,8},{8,12},{12,16},{16,20},{20,24},{24,28},{1,5},{5,9},{9,... | collective-permute-start | bytes 393224 | tf_op jit(solution)/shard_map/while/body/eval_jaxpr/ppermute | solution.py:14
  151.0 6.3 %collective-permute-start = (bf16[128,512]{1,0:T(8,128)(2,1)S(1)}, bf16[128,512]{1,0:T(8,128)(2,1)S(1)}, u32[]{:S(2)}, u32[]{:S(2)}) collective-permute-start(bf16[128,512]{1,0:T(8,128)(2,1)S(1)} %convolution_convert_fusion.5), channel_id=1, source_target_pairs={{0,4},{4,8},{8,12},{12,16},{16,20},{20,24},{24,28},{1,5},{5,9},{9,... | collective-permute-start | bytes 393224 | tf_op jit(solution)/shard_map/while/body/eval_jaxpr/ppermute | solution.py:14
  158.1 7.1 %collective-permute-start = (bf16[128,512]{1,0:T(8,128)(2,1)S(1)}, bf16[128,512]{1,0:T(8,128)(2,1)S(1)}, u32[]{:S(2)}, u32[]{:S(2)}) collective-permute-start(bf16[128,512]{1,0:T(8,128)(2,1)S(1)} %convolution_convert_fusion.5), channel_id=1, source_target_pairs={{0,4},{4,8},{8,12},{12,16},{16,20},{20,24},{24,28},{1,5},{5,9},{9,... | collective-permute-start | bytes 393224 | tf_op jit(solution)/shard_map/while/body/eval_jaxpr/ppermute | solution.py:14
  165.2 2.8 copy-start.15
  168.0 12.1 %copy-start.3 = (f32[128,2048]{1,0:T(8,128)}, f32[128,2048]{1,0:T(8,128)S(1)}, u32[]{:S(2)}) copy-start(f32[128,2048]{1,0:T(8,128)S(1)} %fusion.72) | copy-start | bytes 3145732
  168.0 2.6 copy-start.6
  168.0 4.0 copy-start.10
  180.3 7.0 %collective-permute-start.6 = (bf16[128,512]{1,0:T(8,128)(2,1)S(1)}, bf16[128,512]{1,0:T(8,128)(2,1)S(1)}, u32[]{:S(2)}, u32[]{:S(2)}) collective-permute-start(bf16[128,512]{1,0:T(8,128)(2,1)S(1)} %add_convert_fusion.3), channel_id=1, source_target_pairs={{4,0},{8,4},{12,8},{16,12},{20,16},{24,20},{28,24},{5,1},{9,5},{13... | collective-permute-start | bytes 393224 | tf_op jit(solution)/shard_map/ppermute | solution.py:14
  191.7 12.3 %copy-start.2 = (f32[512,512]{1,0:T(8,128)S(1)}, f32[512,512]{1,0:T(8,128)}, u32[]{:S(2)}) copy-start(f32[512,512]{1,0:T(8,128)} %copy-done.1) | copy-start | bytes 3145732
  196.1 7.9 %collective-permute-start.7 = (bf16[128,512]{1,0:T(8,128)(2,1)S(1)}, bf16[128,512]{1,0:T(8,128)(2,1)S(1)}, u32[]{:S(2)}, u32[]{:S(2)}) collective-permute-start(bf16[128,512]{1,0:T(8,128)(2,1)S(1)} %add_convert_fusion.2), channel_id=1, source_target_pairs={{4,0},{8,4},{12,8},{16,12},{20,16},{24,20},{28,24},{5,1},{9,5},{13... | collective-permute-start | bytes 393224 | tf_op jit(solution)/shard_map/ppermute | solution.py:14
  205.8 16.4 %collective-permute-start.9 = (bf16[128,512]{1,0:T(8,128)(2,1)}, bf16[128,512]{1,0:T(8,128)(2,1)}, u32[]{:S(2)}, u32[]{:S(2)}) collective-permute-start(bf16[128,512]{1,0:T(8,128)(2,1)} %convolution_convert_fusion.2), channel_id=1, source_target_pairs={{4,0},{8,4},{12,8},{16,12},{20,16},{24,20},{28,24},{5,1},{9,5},{13... | collective-permute-start | bytes 393224 | tf_op jit(solution)/shard_map/ppermute | solution.py:14
  218.0 7.9 %collective-permute-start.8 = (bf16[128,512]{1,0:T(8,128)(2,1)}, bf16[128,512]{1,0:T(8,128)(2,1)S(1)}, u32[]{:S(2)}, u32[]{:S(2)}) collective-permute-start(bf16[128,512]{1,0:T(8,128)(2,1)} %get-tuple-element.110), channel_id=1, source_target_pairs={{4,0},{8,4},{12,8},{16,12},{20,16},{24,20},{28,24},{5,1},{9,5},{13... | collective-permute-start | bytes 393224 | tf_op jit(solution)/shard_map/ppermute | solution.py:14
  227.6 7.9 %collective-permute-start.1 = (bf16[128,512]{1,0:T(8,128)(2,1)S(1)}, bf16[128,512]{1,0:T(8,128)(2,1)S(1)}, u32[]{:S(2)}, u32[]{:S(2)}) collective-permute-start(bf16[128,512]{1,0:T(8,128)(2,1)S(1)} %convolution_convert_fusion.6), channel_id=1, source_target_pairs={{4,0},{8,4},{12,8},{16,12},{20,16},{24,20},{28,24},{5,1},{9,5},{13... | collective-permute-start | bytes 393224 | tf_op jit(solution)/shard_map/while/body/eval_jaxpr/ppermute | solution.py:14
  236.3 7.2 %collective-permute-start.1 = (bf16[128,512]{1,0:T(8,128)(2,1)S(1)}, bf16[128,512]{1,0:T(8,128)(2,1)S(1)}, u32[]{:S(2)}, u32[]{:S(2)}) collective-permute-start(bf16[128,512]{1,0:T(8,128)(2,1)S(1)} %convolution_convert_fusion.6), channel_id=1, source_target_pairs={{4,0},{8,4},{12,8},{16,12},{20,16},{24,20},{28,24},{5,1},{9,5},{13... | collective-permute-start | bytes 393224 | tf_op jit(solution)/shard_map/while/body/eval_jaxpr/ppermute | solution.py:14
  244.3 7.2 %collective-permute-start.1 = (bf16[128,512]{1,0:T(8,128)(2,1)S(1)}, bf16[128,512]{1,0:T(8,128)(2,1)S(1)}, u32[]{:S(2)}, u32[]{:S(2)}) collective-permute-start(bf16[128,512]{1,0:T(8,128)(2,1)S(1)} %convolution_convert_fusion.6), channel_id=1, source_target_pairs={{4,0},{8,4},{12,8},{16,12},{20,16},{24,20},{28,24},{5,1},{9,5},{13... | collective-permute-start | bytes 393224 | tf_op jit(solution)/shard_map/while/body/eval_jaxpr/ppermute | solution.py:14
  252.2 7.2 %collective-permute-start.1 = (bf16[128,512]{1,0:T(8,128)(2,1)S(1)}, bf16[128,512]{1,0:T(8,128)(2,1)S(1)}, u32[]{:S(2)}, u32[]{:S(2)}) collective-permute-start(bf16[128,512]{1,0:T(8,128)(2,1)S(1)} %convolution_convert_fusion.6), channel_id=1, source_target_pairs={{4,0},{8,4},{12,8},{16,12},{20,16},{24,20},{28,24},{5,1},{9,5},{13... | collective-permute-start | bytes 393224 | tf_op jit(solution)/shard_map/while/body/eval_jaxpr/ppermute | solution.py:14
  260.2 7.2 %collective-permute-start.1 = (bf16[128,512]{1,0:T(8,128)(2,1)S(1)}, bf16[128,512]{1,0:T(8,128)(2,1)S(1)}, u32[]{:S(2)}, u32[]{:S(2)}) collective-permute-start(bf16[128,512]{1,0:T(8,128)(2,1)S(1)} %convolution_convert_fusion.6), channel_id=1, source_target_pairs={{4,0},{8,4},{12,8},{16,12},{20,16},{24,20},{28,24},{5,1},{9,5},{13... | collective-permute-start | bytes 393224 | tf_op jit(solution)/shard_map/while/body/eval_jaxpr/ppermute | solution.py:14
  268.2 7.2 %collective-permute-start.1 = (bf16[128,512]{1,0:T(8,128)(2,1)S(1)}, bf16[128,512]{1,0:T(8,128)(2,1)S(1)}, u32[]{:S(2)}, u32[]{:S(2)}) collective-permute-start(bf16[128,512]{1,0:T(8,128)(2,1)S(1)} %convolution_convert_fusion.6), channel_id=1, source_target_pairs={{4,0},{8,4},{12,8},{16,12},{20,16},{24,20},{28,24},{5,1},{9,5},{13... | collective-permute-start | bytes 393224 | tf_op jit(solution)/shard_map/while/body/eval_jaxpr/ppermute | solution.py:14
  276.1 7.2 %collective-permute-start.1 = (bf16[128,512]{1,0:T(8,128)(2,1)S(1)}, bf16[128,512]{1,0:T(8,128)(2,1)S(1)}, u32[]{:S(2)}, u32[]{:S(2)}) collective-permute-start(bf16[128,512]{1,0:T(8,128)(2,1)S(1)} %convolution_convert_fusion.6), channel_id=1, source_target_pairs={{4,0},{8,4},{12,8},{16,12},{20,16},{24,20},{28,24},{5,1},{9,5},{13... | collective-permute-start | bytes 393224 | tf_op jit(solution)/shard_map/while/body/eval_jaxpr/ppermute | solution.py:14
  283.4 3.1 copy-start.7
  286.5 1.7 copy-start.13
  286.5 2.5 copy-start.4
  289.0 3.7 copy-start.12
  289.0 137.8 %all-gather.3.cloned.1.call-start = ((), (), s32[]{:S(2)}) async-start(), calls=%async_computation.3 | async-start | bytes 5242880 | tf_op jit(solution)/shard_map/all_gather | solution.py:131
  289.0 2.5 copy-start.14
  291.6 9.2 %copy-start.5 = (f32[128,2048]{1,0:T(8,128)S(1)}, f32[128,2048]{1,0:T(8,128)}, u32[]{:S(2)}) copy-start(f32[128,2048]{1,0:T(8,128)} %fusion.43) | copy-start | bytes 3145732
  296.1 11.5 %all-to-all-start = ((bf16[2,128,512]{1,0,2:T(2,128)(2,1)}), bf16[2,128,512]{1,0,2:T(2,128)(2,1)}, u32[]{:S(2)}, u32[]{:S(2)}) async-start(bf16[2,128,512]{1,0,2:T(2,128)(2,1)} %copy.10), calls=%async_computation | async-start | bytes 524288 | tf_op jit(solution)/shard_map/all_to_all | solution.py:127
  307.6 42.5 %all-to-all-start.1 = ((bf16[2,128,2048]{1,0,2:T(2,128)(2,1)}), bf16[2,128,2048]{1,0,2:T(2,128)(2,1)S(1)}, u32[]{:S(2)}, u32[]{:S(2)}) async-start(bf16[2,128,2048]{1,0,2:T(2,128)(2,1)} %copy.13), calls=%async_computation.1 | async-start | bytes 2097152 | tf_op jit(solution)/shard_map/all_to_all | solution.py:128
  351.3 75.4 %copy-start.8 = (bf16[2,512,128]{1,2,0:T(8,128)(2,1)S(1)}, bf16[2,512,128]{1,2,0:T(8,128)(2,1)}, u32[]{:S(2)}) copy-start(bf16[2,512,128]{1,2,0:T(8,128)(2,1)} %all_to_all.29) | copy-start | bytes 786436
Sparse Core Ops, SparseCore 0:
  11.6 56.1 all-reduce.1
  289.1 52.3 all-gather.4
  343.7 83.0 all-gather.2
where the time goes:
time: 439 us; the launch traced here: 438 us
  waiting for transfers between devices  237 us (54%)
  matrix products  86.1 us (20%)
  starting transfers between devices  74.1 us (17%)
  between operations  14.2 us (3%)
  local copies, waits for them, and re-layouts  13.4 us (3%)
  other arithmetic  12.5 us (3%)
    all_gather x1, waiting for transfers between devices, shards(): lax.all_gather(delta_all, 'dp', axis=1, tiled=True)  72 us
    ppermute x22, starting transfers between devices, shifted(): return lax.ppermute(block, axis, route)  65.9 us
    ppermute x22, waiting for transfers between devices, shifted(): return lax.ppermute(block, axis, route)  65.8 us
    psum x1, waiting for transfers between devices, shards(): start = lax.psum(picked.astype(jnp.bfloat16), 'depth').astype(jnp.float32)  57.6 us
    all_to_all x1, waiting for transfers between devices, shards(): lax.all_to_all(hidden_all, 'dp', split_axis=2, concat_axis=1, tiled=True)  37 us
    dot_general x7, matrix products, layer_adjoint(): lax.dot_general(delta, weight_up, (((1,), (1,)), ((), ())), preferred_ele...  26.4 us
    dot_general x7, matrix products, layer_forward(): jnp.dot(hidden, weight_down, preferred_element_type=jnp.float32)  21.2 us
  transfers between devices with their start and end apart: 27, of which 22 were waited for; matrix products, arithmetic and copies ran while one was open for 9% of the time, Pallas kernels for 0%

commit v1 on v0

--- a/solution.py
+++ b/solution.py
@@ -56,7 +56,9 @@
     inside = (local_ids >= 0) & (local_ids < vocab_rows)
     picked = jnp.take(embedding, jnp.clip(local_ids, 0, vocab_rows - 1), axis=0)
     picked = jnp.where(inside[:, None], picked, jnp.zeros_like(picked)).astype(jnp.float32)
-    start = lax.psum(picked.astype(jnp.bfloat16), "depth").astype(jnp.float32)
+    start = jnp.sum(lax.all_gather(picked.astype(jnp.bfloat16), "depth"), axis=0).astype(
+        jnp.float32
+    )
     matrix = coarse_matrix(w_up, w_down)
     transposed = matrix.T
     zeros = jnp.zeros_like(start)

time: 439 us -> 410 us (0.934)
  waiting for transfers between devices: 237 us -> 209 us
    psum x1 -> x0, waiting for transfers between devices: 57.6 us -> none  [shards(): start = lax.psum(picked.astype(jnp.bfloat16), 'depth').astype(jnp.float32)]
    all_gather x0 -> x1, waiting for transfers between devices: none -> 26.4 us  [shards(): lax.all_gather(picked.astype(jnp.bfloat16), 'depth')]
where the time goes in v1:
time: 410 us; the launch traced here: 408 us
  waiting for transfers between devices  209 us (51%)
  matrix products  86.6 us (21%)
  starting transfers between devices  74.6 us (18%)
  between operations  14.2 us (3%)
  other arithmetic  12.4 us (3%)
  local copies, waits for them, and re-layouts  11.5 us (3%)
    all_gather x1, waiting for transfers between devices, shards(): lax.all_gather(delta_all, 'dp', axis=1, tiled=True)  74.1 us
    ppermute x22, starting transfers between devices, shifted(): return lax.ppermute(block, axis, route)  66.4 us
    ppermute x22, waiting for transfers between devices, shifted(): return lax.ppermute(block, axis, route)  65.7 us
    all_to_all x1, waiting for transfers between devices, shards(): lax.all_to_all(hidden_all, 'dp', split_axis=2, concat_axis=1, tiled=True)  39.5 us
    dot_general x7, matrix products, layer_adjoint(): lax.dot_general(delta, weight_up, (((1,), (1,)), ((), ())), preferred_ele...  27.1 us
    all_gather x1, waiting for transfers between devices, shards(): lax.all_gather(picked.astype(jnp.bfloat16), 'depth')  26.4 us
    dot_general x7, matrix products, layer_forward(): jnp.dot(hidden, weight_down, preferred_element_type=jnp.float32)  21.2 us
  transfers between devices with their start and end apart: 27, of which 22 were waited for; matrix products, arithmetic and copies ran while one was open for 9% of the time, Pallas kernels for 0%

profile of v1, /device:TPU:0, one launch (start us, length us, event | category | flops | bytes accessed | tf_op | source)
XLA Modules:
  0.0 408.4 jit_solution(5834494442625079593)
XLA Ops:
  10.2 26.4 %all-gather.4.cloned.1.call-done = bf16[8,128,512]{2,1,0:T(8,128)(2,1)} async-done(((bf16[1,128,512]{2,1,0:T(8,128)(2,1)}), bf16[8,128,512]{2,1,0:T(8,128)(2,1)}) %all-gather.4.cloned.1.call-update) | async-done | bytes 1048592 | tf_op jit(solution)/shard_map/all_gather | solution.py:59
  36.6 1.4 reduce_sum.147
  38.1 3.1 multiply_reduce_fusion.13
  41.2 3.0 fusion.115
  44.2 2.2 collective-permute-start.2
  46.4 4.4 %fusion.27 = f32[512,512]{1,0:T(8,128)} fusion(bf16[2,2048,512]{2,1,0:T(8,128)(2,1)} %param.12, bf16[2,512,2048]{2,1,0:T(8,128)(2,1)} %param.11), kind=kOutput, calls=%fused_computation.40 | convolution fusion | flops 1073741824 | bytes 5242880 | tf_op jit(solution)/shard_map/dot_general | solution.py:44
  50.9 3.1 multiply_reduce_fusion.11
  54.0 3.7 fusion.118
  57.7 3.3 collective-permute-start.3
  61.0 3.7 convert_add_fusion
  65.6 3.7 multiply_reduce_fusion.9
  69.4 4.0 fusion.121
  73.3 4.0 collective-permute-start.4
  77.3 1.5 fusion.245
  78.8 4.5 %collective-permute-start.5 = (f32[128,512]{1,0:T(8,128)}, f32[128,512]{1,0:T(8,128)S(1)}, u32[]{:S(2)}, u32[]{:S(2)}) collective-permute-start(f32[128,512]{1,0:T(8,128)} %fusion.245), channel_id=1, source_target_pairs={{0,4},{4,8},{8,12},{12,16},{16,20},{20,24},{24,28},{1,5},{5,9},{9,... | collective-permute-start | bytes 786440 | tf_op jit(solution)/shard_map/ppermute | solution.py:14
  84.5 50.3 %while.22 = (s32[]{:T(128)}, f32[128,512]{1,0:T(8,128)S(1)}, f32[128,512]{1,0:T(8,128)S(1)}, f32[512,512]{1,0:T(8,128)S(1)}, s32[]{:T(128)}, /*index=5*/s32[]{:T(128)}) while((s32[]{:T(128)}, f32[128,512]{1,0:T(8,128)S(1)}, f32[128,512]{1,0:T(8,128)S(1)}, f32[512,512]{1,0:T(8,128)S(1)}, s32[]{:T(128)}, /*index=5*/s32[]{:T(128)}) %tuple.64), condition=%wide.region_8.9_spmd.clone, body=%wide.region_7.8_spmd.clone.sunk | while | flops 402915328 | bytes 2621559 | solution.py:80
  85.3 5.4 %collective-permute-start = (bf16[128,512]{1,0:T(8,128)(2,1)S(1)}, bf16[128,512]{1,0:T(8,128)(2,1)S(1)}, u32[]{:S(2)}, u32[]{:S(2)}) collective-permute-start(bf16[128,512]{1,0:T(8,128)(2,1)S(1)} %convolution_convert_fusion.5), channel_id=1, source_target_pairs={{0,4},{4,8},{8,12},{12,16},{16,20},{20,24},{24,28},{1,5},{5,9},{9,... | collective-permute-start | bytes 393224 | tf_op jit(solution)/shard_map/while/body/eval_jaxpr/ppermute | solution.py:14
  92.4 5.2 %collective-permute-start = (bf16[128,512]{1,0:T(8,128)(2,1)S(1)}, bf16[128,512]{1,0:T(8,128)(2,1)S(1)}, u32[]{:S(2)}, u32[]{:S(2)}) collective-permute-start(bf16[128,512]{1,0:T(8,128)(2,1)S(1)} %convolution_convert_fusion.5), channel_id=1, source_target_pairs={{0,4},{4,8},{8,12},{12,16},{16,20},{20,24},{24,28},{1,5},{5,9},{9,... | collective-permute-start | bytes 393224 | tf_op jit(solution)/shard_map/while/body/eval_jaxpr/ppermute | solution.py:14
  99.4 5.3 %collective-permute-start = (bf16[128,512]{1,0:T(8,128)(2,1)S(1)}, bf16[128,512]{1,0:T(8,128)(2,1)S(1)}, u32[]{:S(2)}, u32[]{:S(2)}) collective-permute-start(bf16[128,512]{1,0:T(8,128)(2,1)S(1)} %convolution_convert_fusion.5), channel_id=1, source_target_pairs={{0,4},{4,8},{8,12},{12,16},{16,20},{20,24},{24,28},{1,5},{5,9},{9,... | collective-permute-start | bytes 393224 | tf_op jit(solution)/shard_map/while/body/eval_jaxpr/ppermute | solution.py:14
  106.5 5.3 %collective-permute-start = (bf16[128,512]{1,0:T(8,128)(2,1)S(1)}, bf16[128,512]{1,0:T(8,128)(2,1)S(1)}, u32[]{:S(2)}, u32[]{:S(2)}) collective-permute-start(bf16[128,512]{1,0:T(8,128)(2,1)S(1)} %convolution_convert_fusion.5), channel_id=1, source_target_pairs={{0,4},{4,8},{8,12},{12,16},{16,20},{20,24},{24,28},{1,5},{5,9},{9,... | collective-permute-start | bytes 393224 | tf_op jit(solution)/shard_map/while/body/eval_jaxpr/ppermute | solution.py:14
  113.6 5.3 %collective-permute-start = (bf16[128,512]{1,0:T(8,128)(2,1)S(1)}, bf16[128,512]{1,0:T(8,128)(2,1)S(1)}, u32[]{:S(2)}, u32[]{:S(2)}) collective-permute-start(bf16[128,512]{1,0:T(8,128)(2,1)S(1)} %convolution_convert_fusion.5), channel_id=1, source_target_pairs={{0,4},{4,8},{8,12},{12,16},{16,20},{20,24},{24,28},{1,5},{5,9},{9,... | collective-permute-start | bytes 393224 | tf_op jit(solution)/shard_map/while/body/eval_jaxpr/ppermute | solution.py:14
  120.7 5.3 %collective-permute-start = (bf16[128,512]{1,0:T(8,128)(2,1)S(1)}, bf16[128,512]{1,0:T(8,128)(2,1)S(1)}, u32[]{:S(2)}, u32[]{:S(2)}) collective-permute-start(bf16[128,512]{1,0:T(8,128)(2,1)S(1)} %convolution_convert_fusion.5), channel_id=1, source_target_pairs={{0,4},{4,8},{8,12},{12,16},{16,20},{20,24},{24,28},{1,5},{5,9},{9,... | collective-permute-start | bytes 393224 | tf_op jit(solution)/shard_map/while/body/eval_jaxpr/ppermute | solution.py:14
  127.7 6.1 %collective-permute-start = (bf16[128,512]{1,0:T(8,128)(2,1)S(1)}, bf16[128,512]{1,0:T(8,128)(2,1)S(1)}, u32[]{:S(2)}, u32[]{:S(2)}) collective-permute-start(bf16[128,512]{1,0:T(8,128)(2,1)S(1)} %convolution_convert_fusion.5), channel_id=1, source_target_pairs={{0,4},{4,8},{8,12},{12,16},{16,20},{20,24},{24,28},{1,5},{5,9},{9,... | collective-permute-start | bytes 393224 | tf_op jit(solution)/shard_map/while/body/eval_jaxpr/ppermute | solution.py:14
  135.0 2.2 fusion.72
  138.3 1.9 copy-done.5
  140.3 1.5 fusion.43
  141.7 4.2 %multiply_reduce_fusion.6 = (f32[128]{0:T(128)S(1)}, f32[128,512]{1,0:T(8,128)S(1)}) fusion(f32[128,512]{1,0:T(8,128)S(1)} %get-tuple-element.122, f32[128]{0:T(128)S(1)} %add_rsqrt_fusion, bf16[2,512,2048]{2,1,0:T(8,128)(2,1)} %param.11, bf16[128,512]{1,0:T(8,128)(2,1)S(1)} %copy-done.8, f32[128,2048]{1,0:T(8,128)} %fusion.43, ...), kind=kOutput, calls=%fused_computation.180 | convolution fusion | flops 539426688 | bytes 5899264 | tf_op jit(solution)/shard_map/dot_general | solution.py:34
  145.9 3.9 multiply_reduce_fusion.5
  150.0 1.3 collective-permute-start.6
  151.3 5.7 %collective-permute-done.6 = bf16[128,512]{1,0:T(8,128)(2,1)S(1)} collective-permute-done((bf16[128,512]{1,0:T(8,128)(2,1)S(1)}, bf16[128,512]{1,0:T(8,128)(2,1)S(1)}, u32[]{:S(2)}, u32[]{:S(2)}) %collective-permute-start.6) | collective-permute-done | bytes 131104 | tf_op jit(solution)/shard_map/ppermute | solution.py:14
  157.0 4.2 %multiply_reduce_fusion.4 = (f32[128]{0:T(128)S(1)}, f32[128,512]{1,0:T(8,128)S(1)}) fusion(f32[128,512]{1,0:T(8,128)S(1)} %get-tuple-element.122, f32[128]{0:T(128)S(1)} %add_rsqrt_fusion, bf16[2,512,2048]{2,1,0:T(8,128)(2,1)} %param.11, f32[128,2048]{1,0:T(8,128)} %fusion.43, bf16[2,2048,512]{2,1,0:T(8,128)(2,1)} %param.12, ...), kind=kOutput, calls=%fused_computation.177 | convolution fusion | flops 539688832 | bytes 6030337 | tf_op jit(solution)/shard_map/dot_general | solution.py:34
  161.4 4.3 %multiply_reduce_fusion.3 = (f32[128]{0:T(128)S(1)}, f32[128,512]{1,0:T(8,128)S(1)}) fusion(f32[128,512]{1,0:T(8,128)S(1)} %get-tuple-element.105, f32[128]{0:T(128)S(1)} %add_rsqrt_fusion.1, bf16[2,512,2048]{2,1,0:T(8,128)(2,1)} %param.11, f32[128,2048]{1,0:T(8,128)} %copy-done.3, f32[128,512]{1,0:T(8,128)S(1)} %multiply_add_fusion.9, ...), kind=kOutput, calls=%fused_computation.175 | convolution fusion | flops 539492224 | bytes 6030336 | tf_op jit(solution)/shard_map/dot_general | solution.py:34
  165.8 1.3 collective-permute-start.7
  167.1 6.6 %collective-permute-done.7 = bf16[128,512]{1,0:T(8,128)(2,1)S(1)} collective-permute-done((bf16[128,512]{1,0:T(8,128)(2,1)S(1)}, bf16[128,512]{1,0:T(8,128)(2,1)S(1)}, u32[]{:S(2)}, u32[]{:S(2)}) %collective-permute-start.7) | collective-permute-done | bytes 131104 | tf_op jit(solution)/shard_map/ppermute | solution.py:14
  173.7 1.8 convolution_convert_fusion.2
  176.8 4.8 %multiply_reduce_fusion.2 = (f32[128]{0:T(128)S(1)}, f32[128,512]{1,0:T(8,128)}) fusion(f32[128,512]{1,0:T(8,128)S(1)} %get-tuple-element.122, f32[128]{0:T(128)S(1)} %add_rsqrt_fusion, bf16[2,512,2048]{2,1,0:T(8,128)(2,1)} %param.11, f32[128,2048]{1,0:T(8,128)} %fusion.43, bf16[2,2048,512]{2,1,0:T(8,128)(2,1)} %param.12, ...), kind=kOutput, calls=%fused_computation.173 | convolution fusion | flops 539688832 | bytes 6030337 | tf_op jit(solution)/shard_map/dot_general | solution.py:34
  182.7 4.8 %multiply_reduce_fusion.1 = (f32[128]{0:T(128)S(1)}, f32[128,512]{1,0:T(8,128)}) fusion(f32[128,512]{1,0:T(8,128)S(1)} %get-tuple-element.105, f32[128]{0:T(128)S(1)} %add_rsqrt_fusion.1, bf16[2,512,2048]{2,1,0:T(8,128)(2,1)} %param.11, f32[128,2048]{1,0:T(8,128)} %copy-done.3, f32[128,512]{1,0:T(8,128)S(1)} %multiply_add_fusion.8, ...), kind=kOutput, calls=%fused_computation.171 | convolution fusion | flops 539492224 | bytes 6030336 | tf_op jit(solution)/shard_map/dot_general | solution.py:34
  188.6 1.5 collective-permute-start.8
  191.2 1.6 copy.12
  192.8 3.6 collective-permute-done.8
  197.4 56.4 %while.23 = (s32[]{:T(128)}, f32[128,512]{1,0:T(8,128)S(1)}, f32[128,512]{1,0:T(8,128)S(1)}, f32[512,512]{1,0:T(8,128)S(1)}, s32[]{:T(128)}, /*index=5*/s32[]{:T(128)}) while((s32[]{:T(128)}, f32[128,512]{1,0:T(8,128)S(1)}, f32[128,512]{1,0:T(8,128)S(1)}, f32[512,512]{1,0:T(8,128)S(1)}, s32[]{:T(128)}, ...), condition=%wide.region_18.19_spmd.clone, body=%wide.region_17.18_spmd.clone.sunk | while | flops 402915328 | bytes 2621559 | solution.py:114
  198.2 1.3 collective-permute-start.1
  199.5 6.6 %collective-permute-done.1 = bf16[128,512]{1,0:T(8,128)(2,1)S(1)} collective-permute-done((bf16[128,512]{1,0:T(8,128)(2,1)S(1)}, bf16[128,512]{1,0:T(8,128)(2,1)S(1)}, u32[]{:S(2)}, u32[]{:S(2)}) %collective-permute-start.1) | collective-permute-done | bytes 131104 | tf_op jit(solution)/shard_map/while/body/eval_jaxpr/ppermute | solution.py:14
  206.8 1.3 collective-permute-start.1
  208.1 5.9 %collective-permute-done.1 = bf16[128,512]{1,0:T(8,128)(2,1)S(1)} collective-permute-done((bf16[128,512]{1,0:T(8,128)(2,1)S(1)}, bf16[128,512]{1,0:T(8,128)(2,1)S(1)}, u32[]{:S(2)}, u32[]{:S(2)}) %collective-permute-start.1) | collective-permute-done | bytes 131104 | tf_op jit(solution)/shard_map/while/body/eval_jaxpr/ppermute | solution.py:14
  214.8 1.3 collective-permute-start.1
  216.1 5.9 %collective-permute-done.1 = bf16[128,512]{1,0:T(8,128)(2,1)S(1)} collective-permute-done((bf16[128,512]{1,0:T(8,128)(2,1)S(1)}, bf16[128,512]{1,0:T(8,128)(2,1)S(1)}, u32[]{:S(2)}, u32[]{:S(2)}) %collective-permute-start.1) | collective-permute-done | bytes 131104 | tf_op jit(solution)/shard_map/while/body/eval_jaxpr/ppermute | solution.py:14
  222.8 1.3 collective-permute-start.1
  224.1 5.9 %collective-permute-done.1 = bf16[128,512]{1,0:T(8,128)(2,1)S(1)} collective-permute-done((bf16[128,512]{1,0:T(8,128)(2,1)S(1)}, bf16[128,512]{1,0:T(8,128)(2,1)S(1)}, u32[]{:S(2)}, u32[]{:S(2)}) %collective-permute-start.1) | collective-permute-done | bytes 131104 | tf_op jit(solution)/shard_map/while/body/eval_jaxpr/ppermute | solution.py:14
  230.8 1.3 collective-permute-start.1
  232.1 5.9 %collective-permute-done.1 = bf16[128,512]{1,0:T(8,128)(2,1)S(1)} collective-permute-done((bf16[128,512]{1,0:T(8,128)(2,1)S(1)}, bf16[128,512]{1,0:T(8,128)(2,1)S(1)}, u32[]{:S(2)}, u32[]{:S(2)}) %collective-permute-start.1) | collective-permute-done | bytes 131104 | tf_op jit(solution)/shard_map/while/body/eval_jaxpr/ppermute | solution.py:14
  240.0 5.9 %collective-permute-done.1 = bf16[128,512]{1,0:T(8,128)(2,1)S(1)} collective-permute-done((bf16[128,512]{1,0:T(8,128)(2,1)S(1)}, bf16[128,512]{1,0:T(8,128)(2,1)S(1)}, u32[]{:S(2)}, u32[]{:S(2)}) %collective-permute-start.1) | collective-permute-done | bytes 131104 | tf_op jit(solution)/shard_map/while/body/eval_jaxpr/ppermute | solution.py:14
  248.0 5.9 %collective-permute-done.1 = bf16[128,512]{1,0:T(8,128)(2,1)S(1)} collective-permute-done((bf16[128,512]{1,0:T(8,128)(2,1)S(1)}, bf16[128,512]{1,0:T(8,128)(2,1)S(1)}, u32[]{:S(2)}, u32[]{:S(2)}) %collective-permute-start.1) | collective-permute-done | bytes 131104 | tf_op jit(solution)/shard_map/while/body/eval_jaxpr/ppermute | solution.py:14
  254.0 2.9 fusion.20
  259.0 2.5 fusion.22
  263.5 4.6 %all-to-all-start = ((bf16[2,128,512]{1,0,2:T(2,128)(2,1)}), bf16[2,128,512]{1,0,2:T(2,128)(2,1)S(1)}, u32[]{:S(2)}, u32[]{:S(2)}) async-start(bf16[2,128,512]{1,0,2:T(2,128)(2,1)} %copy.10), calls=%async_computation | async-start | bytes 524288 | tf_op jit(solution)/shard_map/all_to_all | solution.py:129
  268.1 1.8 fusion.148
  270.0 2.0 copy.13
  272.0 2.9 all-to-all-done
  274.9 3.5 all-to-all-start.1
  279.5 39.5 %all-to-all-done.1 = bf16[2,128,2048]{1,0,2:T(2,128)(2,1)S(1)} async-done(((bf16[2,128,2048]{1,0,2:T(2,128)(2,1)}), bf16[2,128,2048]{1,0,2:T(2,128)(2,1)S(1)}, u32[]{:S(2)}, u32[]{:S(2)}) %all-to-all-start.1) | async-done | bytes 1048608 | tf_op jit(solution)/shard_map/all_to_all | solution.py:130
  320.3 3.3 fusion.293
  323.6 74.1 %all-gather.6.cloned.1.call-done = bf16[2,512,2048]{2,1,0:T(8,128)(2,1)} async-done(((bf16[2,128,2048]{2,1,0:T(8,128)(2,1)}), bf16[2,512,2048]{2,1,0:T(8,128)(2,1)}) %all-gather.6.cloned.1.call-update) | async-done | bytes 4194320 | tf_op jit(solution)/shard_map/all_gather | solution.py:133
  397.7 4.2 %fusion.292 = f32[2,128,2048]{2,1,0:T(8,128)} fusion(bf16[2,512,128]{1,2,0:T(8,128)(2,1)S(1)} %copy-done.7, bf16[2,512,2048]{2,1,0:T(8,128)(2,1)} %all-gather.6.cloned.1.call-done), kind=kOutput, calls=%fused_computation.267 | convolution fusion | flops 536870912 | bytes 6553600 | tf_op jit(solution)/shard_map/ltd,ltf->ldf/dot_general | solution.py:136
  (121 shorter events, 39.0 us)
Async XLA Ops:
  7.2 1.3 copy-start
  7.2 29.4 %all-gather.4.cloned.1.call-start = ((), (), s32[]{:S(2)}) async-start(), calls=%async_computation.2 | async-start | bytes 1179648 | tf_op jit(solution)/shard_map/all_gather | solution.py:59
  10.1 310.2 %all-gather.8.cloned.1.call-start = ((), (), s32[]{:S(2)}) async-start(), calls=%async_computation.4 | async-start | bytes 1310720 | tf_op jit(solution)/shard_map/all_gather | solution.py:134
  44.2 6.6 %collective-permute-start.2 = (f32[128,512]{1,0:T(8,128)S(1)}, f32[128,512]{1,0:T(8,128)S(1)}, u32[]{:S(2)}, u32[]{:S(2)}) collective-permute-start(f32[128,512]{1,0:T(8,128)S(1)} %fusion.115), channel_id=1, source_target_pairs={{0,4},{4,8},{8,12},{12,16},{16,20},{20,24},{24,28},{1,5},{5,9},{9,... | collective-permute-start | bytes 786440 | tf_op jit(solution)/shard_map/ppermute | solution.py:14
  57.7 7.0 %collective-permute-start.3 = (f32[128,512]{1,0:T(8,128)}, f32[128,512]{1,0:T(8,128)S(1)}, u32[]{:S(2)}, u32[]{:S(2)}) collective-permute-start(f32[128,512]{1,0:T(8,128)} %fusion.118), channel_id=1, source_target_pairs={{0,4},{4,8},{8,12},{12,16},{16,20},{20,24},{24,28},{1,5},{5,9},{9,... | collective-permute-start | bytes 786440 | tf_op jit(solution)/shard_map/ppermute | solution.py:14
  64.7 12.6 %copy-start.1 = (f32[512,512]{1,0:T(8,128)}, f32[512,512]{1,0:T(8,128)S(1)}, u32[]{:S(2)}) copy-start(f32[512,512]{1,0:T(8,128)S(1)} %get-tuple-element.120) | copy-start | bytes 3145732
  64.8 0.8 copy-start.9
  73.3 10.0 %collective-permute-start.4 = (f32[128,512]{1,0:T(8,128)}, f32[128,512]{1,0:T(8,128)}, u32[]{:S(2)}, u32[]{:S(2)}) collective-permute-start(f32[128,512]{1,0:T(8,128)} %fusion.121), channel_id=1, source_target_pairs={{0,4},{4,8},{8,12},{12,16},{16,20},{20,24},{24,28},{1,5},{5,9},{9,... | collective-permute-start | bytes 786440 | tf_op jit(solution)/shard_map/ppermute | solution.py:14
  78.8 5.7 %collective-permute-start.5 = (f32[128,512]{1,0:T(8,128)}, f32[128,512]{1,0:T(8,128)S(1)}, u32[]{:S(2)}, u32[]{:S(2)}) collective-permute-start(f32[128,512]{1,0:T(8,128)} %fusion.245), channel_id=1, source_target_pairs={{0,4},{4,8},{8,12},{12,16},{16,20},{20,24},{24,28},{1,5},{5,9},{9,... | collective-permute-start | bytes 786440 | tf_op jit(solution)/shard_map/ppermute | solution.py:14
  85.3 6.4 %collective-permute-start = (bf16[128,512]{1,0:T(8,128)(2,1)S(1)}, bf16[128,512]{1,0:T(8,128)(2,1)S(1)}, u32[]{:S(2)}, u32[]{:S(2)}) collective-permute-start(bf16[128,512]{1,0:T(8,128)(2,1)S(1)} %convolution_convert_fusion.5), channel_id=1, source_target_pairs={{0,4},{4,8},{8,12},{12,16},{16,20},{20,24},{24,28},{1,5},{5,9},{9,... | collective-permute-start | bytes 393224 | tf_op jit(solution)/shard_map/while/body/eval_jaxpr/ppermute | solution.py:14
  92.4 6.2 %collective-permute-start = (bf16[128,512]{1,0:T(8,128)(2,1)S(1)}, bf16[128,512]{1,0:T(8,128)(2,1)S(1)}, u32[]{:S(2)}, u32[]{:S(2)}) collective-permute-start(bf16[128,512]{1,0:T(8,128)(2,1)S(1)} %convolution_convert_fusion.5), channel_id=1, source_target_pairs={{0,4},{4,8},{8,12},{12,16},{16,20},{20,24},{24,28},{1,5},{5,9},{9,... | collective-permute-start | bytes 393224 | tf_op jit(solution)/shard_map/while/body/eval_jaxpr/ppermute | solution.py:14
  99.4 6.3 %collective-permute-start = (bf16[128,512]{1,0:T(8,128)(2,1)S(1)}, bf16[128,512]{1,0:T(8,128)(2,1)S(1)}, u32[]{:S(2)}, u32[]{:S(2)}) collective-permute-start(bf16[128,512]{1,0:T(8,128)(2,1)S(1)} %convolution_convert_fusion.5), channel_id=1, source_target_pairs={{0,4},{4,8},{8,12},{12,16},{16,20},{20,24},{24,28},{1,5},{5,9},{9,... | collective-permute-start | bytes 393224 | tf_op jit(solution)/shard_map/while/body/eval_jaxpr/ppermute | solution.py:14
  106.5 6.3 %collective-permute-start = (bf16[128,512]{1,0:T(8,128)(2,1)S(1)}, bf16[128,512]{1,0:T(8,128)(2,1)S(1)}, u32[]{:S(2)}, u32[]{:S(2)}) collective-permute-start(bf16[128,512]{1,0:T(8,128)(2,1)S(1)} %convolution_convert_fusion.5), channel_id=1, source_target_pairs={{0,4},{4,8},{8,12},{12,16},{16,20},{20,24},{24,28},{1,5},{5,9},{9,... | collective-permute-start | bytes 393224 | tf_op jit(solution)/shard_map/while/body/eval_jaxpr/ppermute | solution.py:14
  113.6 6.3 %collective-permute-start = (bf16[128,512]{1,0:T(8,128)(2,1)S(1)}, bf16[128,512]{1,0:T(8,128)(2,1)S(1)}, u32[]{:S(2)}, u32[]{:S(2)}) collective-permute-start(bf16[128,512]{1,0:T(8,128)(2,1)S(1)} %convolution_convert_fusion.5), channel_id=1, source_target_pairs={{0,4},{4,8},{8,12},{12,16},{16,20},{20,24},{24,28},{1,5},{5,9},{9,... | collective-permute-start | bytes 393224 | tf_op jit(solution)/shard_map/while/body/eval_jaxpr/ppermute | solution.py:14
  120.7 6.3 %collective-permute-start = (bf16[128,512]{1,0:T(8,128)(2,1)S(1)}, bf16[128,512]{1,0:T(8,128)(2,1)S(1)}, u32[]{:S(2)}, u32[]{:S(2)}) collective-permute-start(bf16[128,512]{1,0:T(8,128)(2,1)S(1)} %convolution_convert_fusion.5), channel_id=1, source_target_pairs={{0,4},{4,8},{8,12},{12,16},{16,20},{20,24},{24,28},{1,5},{5,9},{9,... | collective-permute-start | bytes 393224 | tf_op jit(solution)/shard_map/while/body/eval_jaxpr/ppermute | solution.py:14
  127.7 7.1 %collective-permute-start = (bf16[128,512]{1,0:T(8,128)(2,1)S(1)}, bf16[128,512]{1,0:T(8,128)(2,1)S(1)}, u32[]{:S(2)}, u32[]{:S(2)}) collective-permute-start(bf16[128,512]{1,0:T(8,128)(2,1)S(1)} %convolution_convert_fusion.5), channel_id=1, source_target_pairs={{0,4},{4,8},{8,12},{12,16},{16,20},{20,24},{24,28},{1,5},{5,9},{9,... | collective-permute-start | bytes 393224 | tf_op jit(solution)/shard_map/while/body/eval_jaxpr/ppermute | solution.py:14
  134.9 2.8 copy-start.12
  137.7 8.2 %copy-start.3 = (f32[128,2048]{1,0:T(8,128)}, f32[128,2048]{1,0:T(8,128)S(1)}, u32[]{:S(2)}) copy-start(f32[128,2048]{1,0:T(8,128)S(1)} %fusion.72) | copy-start | bytes 3145732
  137.7 2.6 copy-start.5
  137.7 4.0 copy-start.8
  150.0 7.0 %collective-permute-start.6 = (bf16[128,512]{1,0:T(8,128)(2,1)S(1)}, bf16[128,512]{1,0:T(8,128)(2,1)S(1)}, u32[]{:S(2)}, u32[]{:S(2)}) collective-permute-start(bf16[128,512]{1,0:T(8,128)(2,1)S(1)} %add_convert_fusion.3), channel_id=1, source_target_pairs={{4,0},{8,4},{12,8},{16,12},{20,16},{24,20},{28,24},{5,1},{9,5},{13... | collective-permute-start | bytes 393224 | tf_op jit(solution)/shard_map/ppermute | solution.py:14
  161.4 12.3 %copy-start.2 = (f32[512,512]{1,0:T(8,128)S(1)}, f32[512,512]{1,0:T(8,128)}, u32[]{:S(2)}) copy-start(f32[512,512]{1,0:T(8,128)} %copy-done.1) | copy-start | bytes 3145732
  165.8 7.9 %collective-permute-start.7 = (bf16[128,512]{1,0:T(8,128)(2,1)S(1)}, bf16[128,512]{1,0:T(8,128)(2,1)S(1)}, u32[]{:S(2)}, u32[]{:S(2)}) collective-permute-start(bf16[128,512]{1,0:T(8,128)(2,1)S(1)} %add_convert_fusion.2), channel_id=1, source_target_pairs={{4,0},{8,4},{12,8},{16,12},{20,16},{24,20},{28,24},{5,1},{9,5},{13... | collective-permute-start | bytes 393224 | tf_op jit(solution)/shard_map/ppermute | solution.py:14
  175.5 17.3 %collective-permute-start.9 = (bf16[128,512]{1,0:T(8,128)(2,1)}, bf16[128,512]{1,0:T(8,128)(2,1)}, u32[]{:S(2)}, u32[]{:S(2)}) collective-permute-start(bf16[128,512]{1,0:T(8,128)(2,1)} %convolution_convert_fusion.2), channel_id=1, source_target_pairs={{4,0},{8,4},{12,8},{16,12},{20,16},{24,20},{28,24},{5,1},{9,5},{13... | collective-permute-start | bytes 393224 | tf_op jit(solution)/shard_map/ppermute | solution.py:14
  188.6 7.8 %collective-permute-start.8 = (bf16[128,512]{1,0:T(8,128)(2,1)S(1)}, bf16[128,512]{1,0:T(8,128)(2,1)}, u32[]{:S(2)}, u32[]{:S(2)}) collective-permute-start(bf16[128,512]{1,0:T(8,128)(2,1)S(1)} %get-tuple-element.110), channel_id=1, source_target_pairs={{4,0},{8,4},{12,8},{16,12},{20,16},{24,20},{28,24},{5,1},{9,5},{13... | collective-permute-start | bytes 393224 | tf_op jit(solution)/shard_map/ppermute | solution.py:14
  198.2 7.9 %collective-permute-start.1 = (bf16[128,512]{1,0:T(8,128)(2,1)S(1)}, bf16[128,512]{1,0:T(8,128)(2,1)S(1)}, u32[]{:S(2)}, u32[]{:S(2)}) collective-permute-start(bf16[128,512]{1,0:T(8,128)(2,1)S(1)} %convolution_convert_fusion.6), channel_id=1, source_target_pairs={{4,0},{8,4},{12,8},{16,12},{20,16},{24,20},{28,24},{5,1},{9,5},{13... | collective-permute-start | bytes 393224 | tf_op jit(solution)/shard_map/while/body/eval_jaxpr/ppermute | solution.py:14
  206.8 7.2 %collective-permute-start.1 = (bf16[128,512]{1,0:T(8,128)(2,1)S(1)}, bf16[128,512]{1,0:T(8,128)(2,1)S(1)}, u32[]{:S(2)}, u32[]{:S(2)}) collective-permute-start(bf16[128,512]{1,0:T(8,128)(2,1)S(1)} %convolution_convert_fusion.6), channel_id=1, source_target_pairs={{4,0},{8,4},{12,8},{16,12},{20,16},{24,20},{28,24},{5,1},{9,5},{13... | collective-permute-start | bytes 393224 | tf_op jit(solution)/shard_map/while/body/eval_jaxpr/ppermute | solution.py:14
  214.8 7.2 %collective-permute-start.1 = (bf16[128,512]{1,0:T(8,128)(2,1)S(1)}, bf16[128,512]{1,0:T(8,128)(2,1)S(1)}, u32[]{:S(2)}, u32[]{:S(2)}) collective-permute-start(bf16[128,512]{1,0:T(8,128)(2,1)S(1)} %convolution_convert_fusion.6), channel_id=1, source_target_pairs={{4,0},{8,4},{12,8},{16,12},{20,16},{24,20},{28,24},{5,1},{9,5},{13... | collective-permute-start | bytes 393224 | tf_op jit(solution)/shard_map/while/body/eval_jaxpr/ppermute | solution.py:14
  222.8 7.2 %collective-permute-start.1 = (bf16[128,512]{1,0:T(8,128)(2,1)S(1)}, bf16[128,512]{1,0:T(8,128)(2,1)S(1)}, u32[]{:S(2)}, u32[]{:S(2)}) collective-permute-start(bf16[128,512]{1,0:T(8,128)(2,1)S(1)} %convolution_convert_fusion.6), channel_id=1, source_target_pairs={{4,0},{8,4},{12,8},{16,12},{20,16},{24,20},{28,24},{5,1},{9,5},{13... | collective-permute-start | bytes 393224 | tf_op jit(solution)/shard_map/while/body/eval_jaxpr/ppermute | solution.py:14
  230.8 7.2 %collective-permute-start.1 = (bf16[128,512]{1,0:T(8,128)(2,1)S(1)}, bf16[128,512]{1,0:T(8,128)(2,1)S(1)}, u32[]{:S(2)}, u32[]{:S(2)}) collective-permute-start(bf16[128,512]{1,0:T(8,128)(2,1)S(1)} %convolution_convert_fusion.6), channel_id=1, source_target_pairs={{4,0},{8,4},{12,8},{16,12},{20,16},{24,20},{28,24},{5,1},{9,5},{13... | collective-permute-start | bytes 393224 | tf_op jit(solution)/shard_map/while/body/eval_jaxpr/ppermute | solution.py:14
  238.7 7.2 %collective-permute-start.1 = (bf16[128,512]{1,0:T(8,128)(2,1)S(1)}, bf16[128,512]{1,0:T(8,128)(2,1)S(1)}, u32[]{:S(2)}, u32[]{:S(2)}) collective-permute-start(bf16[128,512]{1,0:T(8,128)(2,1)S(1)} %convolution_convert_fusion.6), channel_id=1, source_target_pairs={{4,0},{8,4},{12,8},{16,12},{20,16},{24,20},{28,24},{5,1},{9,5},{13... | collective-permute-start | bytes 393224 | tf_op jit(solution)/shard_map/while/body/eval_jaxpr/ppermute | solution.py:14
  246.7 7.2 %collective-permute-start.1 = (bf16[128,512]{1,0:T(8,128)(2,1)S(1)}, bf16[128,512]{1,0:T(8,128)(2,1)S(1)}, u32[]{:S(2)}, u32[]{:S(2)}) collective-permute-start(bf16[128,512]{1,0:T(8,128)(2,1)S(1)} %convolution_convert_fusion.6), channel_id=1, source_target_pairs={{4,0},{8,4},{12,8},{16,12},{20,16},{24,20},{28,24},{5,1},{9,5},{13... | collective-permute-start | bytes 393224 | tf_op jit(solution)/shard_map/while/body/eval_jaxpr/ppermute | solution.py:14
  253.9 3.1 copy-start.6
  257.1 1.1 copy-start.10
  257.1 1.9 copy-start.4
  258.9 138.7 %all-gather.6.cloned.1.call-start = ((), (), s32[]{:S(2)}) async-start(), calls=%async_computation.3 | async-start | bytes 5242880 | tf_op jit(solution)/shard_map/all_gather | solution.py:133
  259.0 2.5 copy-start.11
  263.5 11.4 %all-to-all-start = ((bf16[2,128,512]{1,0,2:T(2,128)(2,1)}), bf16[2,128,512]{1,0,2:T(2,128)(2,1)S(1)}, u32[]{:S(2)}, u32[]{:S(2)}) async-start(bf16[2,128,512]{1,0,2:T(2,128)(2,1)} %copy.10), calls=%async_computation | async-start | bytes 524288 | tf_op jit(solution)/shard_map/all_to_all | solution.py:129
  274.9 44.1 %all-to-all-start.1 = ((bf16[2,128,2048]{1,0,2:T(2,128)(2,1)}), bf16[2,128,2048]{1,0,2:T(2,128)(2,1)S(1)}, u32[]{:S(2)}, u32[]{:S(2)}) async-start(bf16[2,128,2048]{1,0,2:T(2,128)(2,1)} %copy.13), calls=%async_computation.1 | async-start | bytes 2097152 | tf_op jit(solution)/shard_map/all_to_all | solution.py:130
  320.3 77.4 %copy-start.7 = (bf16[2,512,128]{1,2,0:T(8,128)(2,1)S(1)}, bf16[2,512,128]{1,2,0:T(8,128)(2,1)}, u32[]{:S(2)}) copy-start(bf16[2,512,128]{1,2,0:T(8,128)(2,1)} %all_to_all.29) | copy-start | bytes 786436
Sparse Core Ops, SparseCore 0:
  10.4 26.0 all-gather.3
  259.1 55.8 all-gather.7
  317.1 80.5 all-gather.5
